TPU v7x, 256 devices: a whole 4x4x8 slice. The times are simulated.
256 devices in a mesh: gx: 64 (over y, z, core), gy: 4 (over x).
Axes of the slice: x: 4, y: 4, z: 8, core: 2. Of those that a mesh axis runs over, the one named last changes fastest.
Arguments:
- members_state: float32 [3, 64, 512, 512], P(None, None, 'gx', 'gy'), may hold values from -6 to 6
- depth_level: int32 [512, 512], P('gx', 'gy'), may hold values from 1 to 8
- land_mask: int32 [512, 512], P('gx', 'gy'), may hold values 0 or 1
- obs_cells: int32 [64, 4, 256], P('gx', 'gy'), may hold values from 0 to 1023
- obs_values: float32 [64, 4, 256], P('gx', 'gy'), may hold values from -6 to 6
- obs_error: float32 [64, 4, 256], P('gx', 'gy'), may hold values from 2 to 8
Outputs:
- analysis: float32 [3, 64, 512, 512], P(None, None, 'gx', 'gy')
Inputs may be any that keep to these rules, and one draw needn't show every extreme that they name: Each value of obs_cells is the row-major index of a cell within the 8 x 128 block held by the device at the same position along gx and gy.
All inputs are finite; a program needn't handle non-finite values. No bound on the sum of `land_mask` on one device may be relied on, other than what follows from the above.
Results may differ from a plain program's by a relative error of at most 0.00005.
Values sent between devices are 32-bit elements; how exact they have to be, the bound alone decides.
No kernel may reach another device: no remote copies, remote signals or barrier semaphores. Data moves between devices by JAX's collectives and lax.ppermute only.
A program may use at most 64 MiB of HBM per device.

v0:
```python
import jax
import jax.numpy as jnp
from jax import lax
from jax.sharding import PartitionSpec as P


def extended(block, sides, width):
    for axis, dim in sides:
        count = lax.axis_size(axis)
        forward = [(i, i + 1) for i in range(count - 1)]
        backward = [(target, source) for source, target in forward]
        low = lax.ppermute(
            lax.slice_in_dim(block, block.shape[dim] - width, None, axis=dim), axis, forward
        )
        high = lax.ppermute(lax.slice_in_dim(block, 0, width, axis=dim), axis, backward)
        block = jnp.concatenate([low, block, high], axis=dim)
    return block


def height_tendency(padded, geo):
    h = padded[0]
    u = padded[1]
    v = padded[2]
    depth = geo[0]
    mask = geo[1][1:-1, 1:-1]
    east = depth * u
    north = depth * v

    def along_x(a):
        return (a[:, 2:, 1:-1] - a[:, :-2, 1:-1]) * 0.5

    def along_y(a):
        return (a[:, 1:-1, 2:] - a[:, 1:-1, :-2]) * 0.5

    def laplace(a):
        return (
            a[:, 2:, 1:-1]
            + a[:, :-2, 1:-1]
            + a[:, 1:-1, 2:]
            + a[:, 1:-1, :-2]
            - 4.0 * a[:, 1:-1, 1:-1]
        )

    def inner(a):
        return a[:, 1:-1, 1:-1]

    dh = -along_x(east) - along_y(north) + 0.05 * laplace(h)
    du = -along_x(h) + 0.2 * inner(v) + 0.05 * laplace(u)
    dv = -along_y(h) - 0.2 * inner(u) + 0.05 * laplace(v)
    return jnp.stack([dh, du, dv]) * mask


def tri_solve(lower, rhs, flipped):
    return lax.linalg.triangular_solve(lower, rhs, left_side=True, lower=True, transpose_a=flipped)


def padded_section(field):
    return extended(field, (("gx", 2), ("gy", 3)), 1)


def local(members_state, depth_level, land_mask, obs_cells, obs_values, obs_error):
    maskf = land_mask.astype(jnp.float32)
    geo = jnp.stack([0.25 * depth_level.astype(jnp.float32) * maskf, maskf])
    geo_wide = extended(geo, (("gx", 1), ("gy", 2)), 3)
    first_offset = members_state * maskf
    single_geometry = geo_wide[:, 2:-2, 2:-2]
    s1 = first_offset + 0.3 * height_tendency(padded_section(first_offset), single_geometry)
    variance_estimate2 = 0.75 * first_offset + 0.25 * (
        s1 + 0.3 * height_tendency(padded_section(s1), single_geometry)
    )
    prior_model_vector = 1.0 / 3.0 * first_offset + 2.0 / 3.0 * (
        variance_estimate2
        + 0.3 * height_tendency(padded_section(variance_estimate2), single_geometry)
    )
    sample_average = jnp.mean(prior_model_vector, axis=1, keepdims=True)
    sample_deviations = prior_model_vector - sample_average
    sample_number = prior_model_vector.shape[1]
    free_elevation_field = prior_model_vector[0].reshape(sample_number, -1)
    measured_data = jnp.take(free_elevation_field, obs_cells.reshape(-1), axis=1)
    obs_mean = jnp.mean(measured_data, axis=0, keepdims=True)
    error = obs_error.reshape(-1)
    scaled = (measured_data - obs_mean) / (error * jnp.sqrt(jnp.float32(sample_number - 1)))
    innovation = (obs_values.reshape(-1) - obs_mean[0]) / error
    gram_part = jnp.dot(scaled, scaled.T, precision=lax.Precision.HIGHEST)
    proj_part = jnp.dot(scaled, innovation, precision=lax.Precision.HIGHEST)
    eye = jnp.eye(sample_number, dtype=jnp.float32)
    gram, projection = lax.psum((gram_part, proj_part), ("gx", "gy"))
    lower = jnp.linalg.cholesky(eye + gram)
    half = tri_solve(lower, projection[:, None], False)
    weights = tri_solve(lower, half, True)[:, 0]
    inverse = tri_solve(lower, eye, False)
    transform = weights[:, None] / jnp.sqrt(jnp.float32(sample_number - 1)) + inverse.T
    mixed = jnp.einsum(
        "km,fkxy->fmxy", transform, sample_deviations, precision=lax.Precision.HIGHEST
    )
    return sample_average + mixed


def solution(mesh):
    placed = (
        P(None, None, "gx", "gy"),
        P("gx", "gy"),
        P("gx", "gy"),
        P("gx", "gy", None),
        P("gx", "gy", None),
        P("gx", "gy", None),
    )
    return jax.shard_map(
        local, mesh=mesh, in_specs=placed, out_specs=P(None, None, "gx", "gy"), check_vma=False
    )
```

profile of v0, /device:TPU:1, one launch (start us, length us, event | category | flops | bytes accessed | tf_op | source)
XLA Modules:
  0.0 180.3 jit_solution(6452280479091019301)
XLA Ops:
  1.4 5.1 %collective-permute-start.1 = (f32[2,3,128]{2,1,0:T(4,128)S(1)}, f32[2,3,128]{2,1,0:T(4,128)S(1)}, u32[]{:S(2)}, u32[]{:S(2)}) collective-permute-start(f32[2,3,128]{2,1,0:T(4,128)S(1)} %get-tuple-element.47), channel_id=1, source_target_pairs={{4,0},{8,4},{12,8},{16,12},{20,16},{24,20},{28,24},{32,28},{36,32}... | collective-permute-start | bytes 9224 | tf_op jit(solution)/shard_map/ppermute | solution.py:15
  6.5 1.9 %collective-permute-start = (f32[2,3,128]{2,1,0:T(4,128)S(1)}, f32[2,3,128]{2,1,0:T(4,128)S(1)}, u32[]{:S(2)}, u32[]{:S(2)}) collective-permute-start(f32[2,3,128]{2,1,0:T(4,128)S(1)} %get-tuple-element.46), channel_id=1, source_target_pairs={{0,4},{4,8},{8,12},{12,16},{16,20},{20,24},{24,28},{28,32},{32,36}... | collective-permute-start | bytes 9224 | tf_op jit(solution)/shard_map/ppermute | solution.py:12
  8.4 1.6 copy.15
  11.7 4.0 %collective-permute-start.2 = (f32[2,14,3]{2,1,0:T(8,128)S(1)}, f32[2,14,3]{2,1,0:T(8,128)S(1)}, u32[]{:S(2)}, u32[]{:S(2)}) collective-permute-start(f32[2,14,3]{2,1,0:T(8,128)S(1)} %get-tuple-element.44), channel_id=1, source_target_pairs={{0,1},{1,2},{2,3},{4,5},{5,6},{6,7},{8,9},{9,10},{10,11},{12,13},{... | collective-permute-start | bytes 1016 | tf_op jit(solution)/shard_map/ppermute | solution.py:12
  15.7 3.0 %collective-permute-start.5 = (f32[3,64,1,128]{1,3,2,0:T(8,128)S(1)}, f32[3,64,1,128]{1,3,2,0:T(8,128)S(1)}, u32[]{:S(2)}, u32[]{:S(2)}) collective-permute-start(f32[3,64,1,128]{1,3,2,0:T(8,128)S(1)} %get-tuple-element.41), channel_id=1, source_target_pairs={{4,0},{8,4},{12,8},{16,12},{20,16},{24,20},{28,24},{32,28},{36,32}... | collective-permute-start | bytes 294920 | tf_op jit(solution)/shard_map/ppermute | solution.py:15
  18.7 2.6 %collective-permute-start.4 = (f32[3,64,1,128]{1,3,2,0:T(8,128)S(1)}, f32[3,64,1,128]{1,3,2,0:T(8,128)S(1)}, u32[]{:S(2)}, u32[]{:S(2)}) collective-permute-start(f32[3,64,1,128]{1,3,2,0:T(8,128)S(1)} %get-tuple-element.40), channel_id=1, source_target_pairs={{0,4},{4,8},{8,12},{12,16},{16,20},{20,24},{24,28},{28,32},{32,36}... | collective-permute-start | bytes 294920 | tf_op jit(solution)/shard_map/ppermute | solution.py:12
  21.4 1.3 collective-permute-done.5
  23.9 1.3 collective-permute-start.7
  25.2 4.0 %collective-permute-start.6 = (f32[3,64,10,1]{1,3,2,0:T(1,128)S(1)}, f32[3,64,10,1]{1,3,2,0:T(1,128)S(1)}, u32[]{:S(2)}, u32[]{:S(2)}) collective-permute-start(f32[3,64,10,1]{1,3,2,0:T(1,128)S(1)} %get-tuple-element.34), channel_id=1, source_target_pairs={{0,1},{1,2},{2,3},{4,5},{5,6},{6,7},{8,9},{9,10},{10,11},{12,13},{... | collective-permute-start | bytes 23048 | tf_op jit(solution)/shard_map/ppermute | solution.py:12
  32.1 1.9 %collective-permute-start.9 = (f32[3,64,1,128]{1,3,2,0:T(8,128)S(1)}, f32[3,64,1,128]{1,3,2,0:T(8,128)S(1)}, u32[]{:S(2)}, u32[]{:S(2)}) collective-permute-start(f32[3,64,1,128]{1,3,2,0:T(8,128)S(1)} %get-tuple-element.39), channel_id=1, source_target_pairs={{4,0},{8,4},{12,8},{16,12},{20,16},{24,20},{28,24},{32,28},{36,32}... | collective-permute-start | bytes 294920 | tf_op jit(solution)/shard_map/ppermute | solution.py:15
  34.1 5.5 %collective-permute-start.8 = (f32[3,64,1,128]{1,3,2,0:T(8,128)S(1)}, f32[3,64,1,128]{1,3,2,0:T(8,128)S(1)}, u32[]{:S(2)}, u32[]{:S(2)}) collective-permute-start(f32[3,64,1,128]{1,3,2,0:T(8,128)S(1)} %get-tuple-element.38), channel_id=1, source_target_pairs={{0,4},{4,8},{8,12},{12,16},{16,20},{20,24},{24,28},{28,32},{32,36}... | collective-permute-start | bytes 294920 | tf_op jit(solution)/shard_map/ppermute | solution.py:12
  39.6 1.4 collective-permute-done.9
  42.2 1.3 collective-permute-start.11
  43.5 4.5 %collective-permute-start.10 = (f32[3,64,10,1]{1,3,2,0:T(1,128)S(1)}, f32[3,64,10,1]{1,3,2,0:T(1,128)S(1)}, u32[]{:S(2)}, u32[]{:S(2)}) collective-permute-start(f32[3,64,10,1]{1,3,2,0:T(1,128)S(1)} %get-tuple-element.32), channel_id=1, source_target_pairs={{0,1},{1,2},{2,3},{4,5},{5,6},{6,7},{8,9},{9,10},{10,11},{12,13},{... | collective-permute-start | bytes 23048 | tf_op jit(solution)/shard_map/ppermute | solution.py:12
  51.4 1.9 %collective-permute-start.13 = (f32[3,64,1,128]{1,3,2,0:T(8,128)S(1)}, f32[3,64,1,128]{1,3,2,0:T(8,128)S(1)}, u32[]{:S(2)}, u32[]{:S(2)}) collective-permute-start(f32[3,64,1,128]{1,3,2,0:T(8,128)S(1)} %get-tuple-element.37), channel_id=1, source_target_pairs={{4,0},{8,4},{12,8},{16,12},{20,16},{24,20},{28,24},{32,28},{36,32}... | collective-permute-start | bytes 294920 | tf_op jit(solution)/shard_map/ppermute | solution.py:15
  53.3 5.2 %collective-permute-start.12 = (f32[3,64,1,128]{1,3,2,0:T(8,128)S(1)}, f32[3,64,1,128]{1,3,2,0:T(8,128)S(1)}, u32[]{:S(2)}, u32[]{:S(2)}) collective-permute-start(f32[3,64,1,128]{1,3,2,0:T(8,128)S(1)} %get-tuple-element.36), channel_id=1, source_target_pairs={{0,4},{4,8},{8,12},{12,16},{16,20},{20,24},{24,28},{28,32},{32,36}... | collective-permute-start | bytes 294920 | tf_op jit(solution)/shard_map/ppermute | solution.py:12
  58.6 1.4 collective-permute-done.13
  62.5 4.5 %collective-permute-start.14 = (f32[3,64,10,1]{1,3,2,0:T(1,128)S(1)}, f32[3,64,10,1]{1,3,2,0:T(1,128)S(1)}, u32[]{:S(2)}, u32[]{:S(2)}) collective-permute-start(f32[3,64,10,1]{1,3,2,0:T(1,128)S(1)} %get-tuple-element.30), channel_id=1, source_target_pairs={{0,1},{1,2},{2,3},{4,5},{5,6},{6,7},{8,9},{9,10},{10,11},{12,13},{... | collective-permute-start | bytes 23048 | tf_op jit(solution)/shard_map/ppermute | solution.py:12
  69.5 1.7 fusion.77
  73.0 91.1 %all-reduce = (f32[64,64]{1,0:T(8,128)S(1)}, f32[64]{0:T(128)S(1)}) all-reduce(f32[64,64]{1,0:T(8,128)S(1)} %fusion.83, f32[64]{0:T(128)S(1)} %convolution_bitcast_fusion.2), channel_id=1, replica_groups=mesh['gx'=64,'gy'=4] {'gx','gy'}, use_global_device_ids=true, to_apply=%region_2.3 | all-reduce | flops 4160 | bytes 33280 | tf_op jit(solution)/shard_map/psum | solution.py:87
  164.2 5.8 %cholesky.18 = f32[64,64]{1,0:T(8,128)S(1)} custom-call(f32[64,64]{1,0:T(8,128)S(1)} %fusion.74), custom_call_target="Cholesky" | custom-call | tf_op jit(solution)/shard_map/jit(cholesky)/cholesky | solution.py:88
  171.4 4.9 %custom-call.10 = f32[1,64,64]{1,2,0:T(8,128)S(1)} custom-call(f32[1,64,64]{2,1,0:T(8,128)S(1)} %fusion.70), custom_call_target="InvertDiagBlocksLowerTriangular" | custom-call | tf_op jit(solution)/shard_map/triangular_solve | solution.py:54
  176.9 2.1 %fusion.15 = f32[3,64,8,128]{3,1,2,0:T(8,128)S(1)} fusion(f32[64,64,1,1]{1,0,3,2:T(8,128)S(1)} %fusion.18, f32[3,64,8,128]{1,3,2,0:T(8,128)S(1)} %get-tuple-element.8, f32[3,8,128]{2,1,0:T(8,128)S(1)} %broadcast_multiply_fusion.7), kind=kOutput, calls=%fused_computation.20 | convolution fusion | flops 151388160 | bytes 1601536 | tf_op jit(solution)/shard_map/km,fkxy->fmxy/dot_general | solution.py:93
  179.0 1.3 copy.19
  (73 shorter events, 20.3 us)
Async XLA Ops:
  1.4 8.9 %collective-permute-start.1 = (f32[2,3,128]{2,1,0:T(4,128)S(1)}, f32[2,3,128]{2,1,0:T(4,128)S(1)}, u32[]{:S(2)}, u32[]{:S(2)}) collective-permute-start(f32[2,3,128]{2,1,0:T(4,128)S(1)} %get-tuple-element.47), channel_id=1, source_target_pairs={{4,0},{8,4},{12,8},{16,12},{20,16},{24,20},{28,24},{32,28},{36,32}... | collective-permute-start | bytes 9224 | tf_op jit(solution)/shard_map/ppermute | solution.py:15
  6.5 3.8 %collective-permute-start = (f32[2,3,128]{2,1,0:T(4,128)S(1)}, f32[2,3,128]{2,1,0:T(4,128)S(1)}, u32[]{:S(2)}, u32[]{:S(2)}) collective-permute-start(f32[2,3,128]{2,1,0:T(4,128)S(1)} %get-tuple-element.46), channel_id=1, source_target_pairs={{0,4},{4,8},{8,12},{12,16},{16,20},{20,24},{24,28},{28,32},{32,36}... | collective-permute-start | bytes 9224 | tf_op jit(solution)/shard_map/ppermute | solution.py:12
  10.4 10.9 %collective-permute-start.3 = (f32[2,14,3]{2,1,0:T(8,128)S(1)}, f32[2,14,3]{2,1,0:T(8,128)S(1)}, u32[]{:S(2)}, u32[]{:S(2)}) collective-permute-start(f32[2,14,3]{2,1,0:T(8,128)S(1)} %get-tuple-element.45), channel_id=1, source_target_pairs={{1,0},{2,1},{3,2},{5,4},{6,5},{7,6},{9,8},{10,9},{11,10},{13,12},{... | collective-permute-start | bytes 1016 | tf_op jit(solution)/shard_map/ppermute | solution.py:15
  11.7 9.6 %collective-permute-start.2 = (f32[2,14,3]{2,1,0:T(8,128)S(1)}, f32[2,14,3]{2,1,0:T(8,128)S(1)}, u32[]{:S(2)}, u32[]{:S(2)}) collective-permute-start(f32[2,14,3]{2,1,0:T(8,128)S(1)} %get-tuple-element.44), channel_id=1, source_target_pairs={{0,1},{1,2},{2,3},{4,5},{5,6},{6,7},{8,9},{9,10},{10,11},{12,13},{... | collective-permute-start | bytes 1016 | tf_op jit(solution)/shard_map/ppermute | solution.py:12
  15.7 7.0 %collective-permute-start.5 = (f32[3,64,1,128]{1,3,2,0:T(8,128)S(1)}, f32[3,64,1,128]{1,3,2,0:T(8,128)S(1)}, u32[]{:S(2)}, u32[]{:S(2)}) collective-permute-start(f32[3,64,1,128]{1,3,2,0:T(8,128)S(1)} %get-tuple-element.41), channel_id=1, source_target_pairs={{4,0},{8,4},{12,8},{16,12},{20,16},{24,20},{28,24},{32,28},{36,32}... | collective-permute-start | bytes 294920 | tf_op jit(solution)/shard_map/ppermute | solution.py:15
  18.7 5.2 %collective-permute-start.4 = (f32[3,64,1,128]{1,3,2,0:T(8,128)S(1)}, f32[3,64,1,128]{1,3,2,0:T(8,128)S(1)}, u32[]{:S(2)}, u32[]{:S(2)}) collective-permute-start(f32[3,64,1,128]{1,3,2,0:T(8,128)S(1)} %get-tuple-element.40), channel_id=1, source_target_pairs={{0,4},{4,8},{8,12},{12,16},{16,20},{20,24},{24,28},{28,32},{32,36}... | collective-permute-start | bytes 294920 | tf_op jit(solution)/shard_map/ppermute | solution.py:12
  23.9 5.5 %collective-permute-start.7 = (f32[3,64,10,1]{1,3,2,0:T(1,128)S(1)}, f32[3,64,10,1]{1,3,2,0:T(1,128)S(1)}, u32[]{:S(2)}, u32[]{:S(2)}) collective-permute-start(f32[3,64,10,1]{1,3,2,0:T(1,128)S(1)} %get-tuple-element.35), channel_id=1, source_target_pairs={{1,0},{2,1},{3,2},{5,4},{6,5},{7,6},{9,8},{10,9},{11,10},{13,12},{... | collective-permute-start | bytes 23048 | tf_op jit(solution)/shard_map/ppermute | solution.py:15
  25.2 4.8 %collective-permute-start.6 = (f32[3,64,10,1]{1,3,2,0:T(1,128)S(1)}, f32[3,64,10,1]{1,3,2,0:T(1,128)S(1)}, u32[]{:S(2)}, u32[]{:S(2)}) collective-permute-start(f32[3,64,10,1]{1,3,2,0:T(1,128)S(1)} %get-tuple-element.34), channel_id=1, source_target_pairs={{0,1},{1,2},{2,3},{4,5},{5,6},{6,7},{8,9},{9,10},{10,11},{12,13},{... | collective-permute-start | bytes 23048 | tf_op jit(solution)/shard_map/ppermute | solution.py:12
  32.1 16.0 %copy-start = (s32[1,1,256]{2,1,0:T(1,128)S(1)}, s32[1,1,256]{2,1,0:T(1,128)}, u32[]{:S(2)}) copy-start(s32[1,1,256]{2,1,0:T(1,128)} %param.9) | copy-start | bytes 3076
  32.1 8.9 %collective-permute-start.9 = (f32[3,64,1,128]{1,3,2,0:T(8,128)S(1)}, f32[3,64,1,128]{1,3,2,0:T(8,128)S(1)}, u32[]{:S(2)}, u32[]{:S(2)}) collective-permute-start(f32[3,64,1,128]{1,3,2,0:T(8,128)S(1)} %get-tuple-element.39), channel_id=1, source_target_pairs={{4,0},{8,4},{12,8},{16,12},{20,16},{24,20},{28,24},{32,28},{36,32}... | collective-permute-start | bytes 294920 | tf_op jit(solution)/shard_map/ppermute | solution.py:15
  34.1 8.1 %collective-permute-start.8 = (f32[3,64,1,128]{1,3,2,0:T(8,128)S(1)}, f32[3,64,1,128]{1,3,2,0:T(8,128)S(1)}, u32[]{:S(2)}, u32[]{:S(2)}) collective-permute-start(f32[3,64,1,128]{1,3,2,0:T(8,128)S(1)} %get-tuple-element.38), channel_id=1, source_target_pairs={{0,4},{4,8},{8,12},{12,16},{16,20},{20,24},{24,28},{28,32},{32,36}... | collective-permute-start | bytes 294920 | tf_op jit(solution)/shard_map/ppermute | solution.py:12
  42.2 5.9 %collective-permute-start.11 = (f32[3,64,10,1]{1,3,2,0:T(1,128)S(1)}, f32[3,64,10,1]{1,3,2,0:T(1,128)S(1)}, u32[]{:S(2)}, u32[]{:S(2)}) collective-permute-start(f32[3,64,10,1]{1,3,2,0:T(1,128)S(1)} %get-tuple-element.33), channel_id=1, source_target_pairs={{1,0},{2,1},{3,2},{5,4},{6,5},{7,6},{9,8},{10,9},{11,10},{13,12},{... | collective-permute-start | bytes 23048 | tf_op jit(solution)/shard_map/ppermute | solution.py:15
  43.5 5.4 %collective-permute-start.10 = (f32[3,64,10,1]{1,3,2,0:T(1,128)S(1)}, f32[3,64,10,1]{1,3,2,0:T(1,128)S(1)}, u32[]{:S(2)}, u32[]{:S(2)}) collective-permute-start(f32[3,64,10,1]{1,3,2,0:T(1,128)S(1)} %get-tuple-element.32), channel_id=1, source_target_pairs={{0,1},{1,2},{2,3},{4,5},{5,6},{6,7},{8,9},{9,10},{10,11},{12,13},{... | collective-permute-start | bytes 23048 | tf_op jit(solution)/shard_map/ppermute | solution.py:12
  51.4 8.6 %collective-permute-start.13 = (f32[3,64,1,128]{1,3,2,0:T(8,128)S(1)}, f32[3,64,1,128]{1,3,2,0:T(8,128)S(1)}, u32[]{:S(2)}, u32[]{:S(2)}) collective-permute-start(f32[3,64,1,128]{1,3,2,0:T(8,128)S(1)} %get-tuple-element.37), channel_id=1, source_target_pairs={{4,0},{8,4},{12,8},{16,12},{20,16},{24,20},{28,24},{32,28},{36,32}... | collective-permute-start | bytes 294920 | tf_op jit(solution)/shard_map/ppermute | solution.py:15
  53.3 7.8 %collective-permute-start.12 = (f32[3,64,1,128]{1,3,2,0:T(8,128)S(1)}, f32[3,64,1,128]{1,3,2,0:T(8,128)S(1)}, u32[]{:S(2)}, u32[]{:S(2)}) collective-permute-start(f32[3,64,1,128]{1,3,2,0:T(8,128)S(1)} %get-tuple-element.36), channel_id=1, source_target_pairs={{0,4},{4,8},{8,12},{12,16},{16,20},{20,24},{24,28},{28,32},{32,36}... | collective-permute-start | bytes 294920 | tf_op jit(solution)/shard_map/ppermute | solution.py:12
  61.2 5.9 %collective-permute-start.15 = (f32[3,64,10,1]{1,3,2,0:T(1,128)S(1)}, f32[3,64,10,1]{1,3,2,0:T(1,128)S(1)}, u32[]{:S(2)}, u32[]{:S(2)}) collective-permute-start(f32[3,64,10,1]{1,3,2,0:T(1,128)S(1)} %get-tuple-element.31), channel_id=1, source_target_pairs={{1,0},{2,1},{3,2},{5,4},{6,5},{7,6},{9,8},{10,9},{11,10},{13,12},{... | collective-permute-start | bytes 23048 | tf_op jit(solution)/shard_map/ppermute | solution.py:15
  62.5 5.4 %collective-permute-start.14 = (f32[3,64,10,1]{1,3,2,0:T(1,128)S(1)}, f32[3,64,10,1]{1,3,2,0:T(1,128)S(1)}, u32[]{:S(2)}, u32[]{:S(2)}) collective-permute-start(f32[3,64,10,1]{1,3,2,0:T(1,128)S(1)} %get-tuple-element.30), channel_id=1, source_target_pairs={{0,1},{1,2},{2,3},{4,5},{5,6},{6,7},{8,9},{9,10},{10,11},{12,13},{... | collective-permute-start | bytes 23048 | tf_op jit(solution)/shard_map/ppermute | solution.py:12
  71.3 1.0 copy-start.1
  71.3 1.0 copy-start.2
where the time goes:
time: 181 us; the launch traced here: 180 us
  blocking collectives  91.1 us (50%)
  starting transfers between devices  49.4 us (27%)
  other arithmetic  21.6 us (12%)
  waiting for transfers between devices  9.98 us (6%)
  local copies, waits for them, and re-layouts  4.53 us (3%)
  matrix products  3.22 us (2%)
    psum x1, blocking collectives, local(): gram, projection = lax.psum((gram_part, proj_part), ('gx', 'gy'))  91.1 us
    ppermute x8, starting transfers between devices, extended(): lax.ppermute(lax.slice_in_dim(block, block.shape[dim] - width, None, axis...  32.4 us
    ppermute x8, starting transfers between devices, extended(): lax.ppermute(lax.slice_in_dim(block, 0, width, axis=dim), axis, backward)  17.1 us
    another operation x3, other arithmetic, local(): lower = jnp.linalg.cholesky(eye + gram)  6.52 us
    ppermute x8, waiting for transfers between devices, extended(): lax.ppermute(lax.slice_in_dim(block, block.shape[dim] - width, None, axis...  5.86 us
    another operation x2, other arithmetic, tri_solve(): lax.linalg.triangular_solve(lower, rhs, left_side=True, lower=True, trans...  5.55 us
    ppermute x8, waiting for transfers between devices, extended(): lax.ppermute(lax.slice_in_dim(block, 0, width, axis=dim), axis, backward)  4.11 us
  transfers between devices with their start and end apart: 16, of which 9 were waited for; matrix products, arithmetic and copies ran while one was open for 1% of the time, Pallas kernels for 0%

commit v1 on v0

--- a/solution.py
+++ b/solution.py
@@ -84,7 +84,7 @@
     gram_part = jnp.dot(scaled, scaled.T, precision=lax.Precision.HIGHEST)
     proj_part = jnp.dot(scaled, innovation, precision=lax.Precision.HIGHEST)
     eye = jnp.eye(sample_number, dtype=jnp.float32)
-    gram, projection = lax.psum((gram_part, proj_part), ("gx", "gy"))
+    gram, projection = lax.psum(lax.psum((gram_part, proj_part), "gx"), "gy")
     lower = jnp.linalg.cholesky(eye + gram)
     half = tri_solve(lower, projection[:, None], False)
     weights = tri_solve(lower, half, True)[:, 0]

time: 181 us -> 358 us (1.98); the launches traced: 180 us -> 351 us
  blocking collectives: 91.1 us -> 262 us
    psum x1 -> x2, blocking collectives: 91.1 us -> 262 us  [local(): gram, projection = lax.psum(lax.psum((gram_part, proj_part), 'gx'), 'gy')]
where the time goes in v1:
time: 358 us; the launch traced here: 351 us
  blocking collectives  262 us (73%)
  starting transfers between devices  49.4 us (14%)
  other arithmetic  21.6 us (6%)
  waiting for transfers between devices  9.98 us (3%)
  local copies, waits for them, and re-layouts  4.53 us (1%)
    psum x2, blocking collectives, local(): gram, projection = lax.psum(lax.psum((gram_part, proj_part), 'gx'), 'gy')  262 us
    ppermute x8, starting transfers between devices, extended(): lax.ppermute(lax.slice_in_dim(block, block.shape[dim] - width, None, axis...  32.4 us
    ppermute x8, starting transfers between devices, extended(): lax.ppermute(lax.slice_in_dim(block, 0, width, axis=dim), axis, backward)  17.1 us
  transfers between devices with their start and end apart: 16, of which 9 were waited for; matrix products, arithmetic and copies ran while one was open for 1% of the time, Pallas kernels for 0%

profile of v1, /device:TPU:1, one launch (start us, length us, event | category | flops | bytes accessed | tf_op | source)
XLA Modules:
  0.0 350.9 jit_solution(17225364352123133400)
XLA Ops:
  1.4 5.1 %collective-permute-start.1 = (f32[2,3,128]{2,1,0:T(4,128)S(1)}, f32[2,3,128]{2,1,0:T(4,128)S(1)}, u32[]{:S(2)}, u32[]{:S(2)}) collective-permute-start(f32[2,3,128]{2,1,0:T(4,128)S(1)} %get-tuple-element.49), channel_id=1, source_target_pairs={{4,0},{8,4},{12,8},{16,12},{20,16},{24,20},{28,24},{32,28},{36,32}... | collective-permute-start | bytes 9224 | tf_op jit(solution)/shard_map/ppermute | solution.py:15
  6.5 1.9 collective-permute-start
  8.4 1.6 copy.15
  11.7 4.0 %collective-permute-start.2 = (f32[2,14,3]{2,1,0:T(8,128)S(1)}, f32[2,14,3]{2,1,0:T(8,128)S(1)}, u32[]{:S(2)}, u32[]{:S(2)}) collective-permute-start(f32[2,14,3]{2,1,0:T(8,128)S(1)} %get-tuple-element.46), channel_id=1, source_target_pairs={{0,1},{1,2},{2,3},{4,5},{5,6},{6,7},{8,9},{9,10},{10,11},{12,13},{... | collective-permute-start | bytes 1016 | tf_op jit(solution)/shard_map/ppermute | solution.py:12
  15.7 3.0 collective-permute-start.5
  18.7 2.6 collective-permute-start.4
  21.4 1.3 collective-permute-done.5
  23.9 1.3 collective-permute-start.7
  25.2 4.0 %collective-permute-start.6 = (f32[3,64,10,1]{1,3,2,0:T(1,128)S(1)}, f32[3,64,10,1]{1,3,2,0:T(1,128)S(1)}, u32[]{:S(2)}, u32[]{:S(2)}) collective-permute-start(f32[3,64,10,1]{1,3,2,0:T(1,128)S(1)} %get-tuple-element.36), channel_id=1, source_target_pairs={{0,1},{1,2},{2,3},{4,5},{5,6},{6,7},{8,9},{9,10},{10,11},{12,13},{... | collective-permute-start | bytes 23048 | tf_op jit(solution)/shard_map/ppermute | solution.py:12
  32.1 1.9 collective-permute-start.9
  34.1 5.5 %collective-permute-start.8 = (f32[3,64,1,128]{1,3,2,0:T(8,128)S(1)}, f32[3,64,1,128]{1,3,2,0:T(8,128)S(1)}, u32[]{:S(2)}, u32[]{:S(2)}) collective-permute-start(f32[3,64,1,128]{1,3,2,0:T(8,128)S(1)} %get-tuple-element.40), channel_id=1, source_target_pairs={{0,4},{4,8},{8,12},{12,16},{16,20},{20,24},{24,28},{28,32},{32,36}... | collective-permute-start | bytes 294920 | tf_op jit(solution)/shard_map/ppermute | solution.py:12
  39.6 1.4 collective-permute-done.9
  43.5 4.5 %collective-permute-start.10 = (f32[3,64,10,1]{1,3,2,0:T(1,128)S(1)}, f32[3,64,10,1]{1,3,2,0:T(1,128)S(1)}, u32[]{:S(2)}, u32[]{:S(2)}) collective-permute-start(f32[3,64,10,1]{1,3,2,0:T(1,128)S(1)} %get-tuple-element.34), channel_id=1, source_target_pairs={{0,1},{1,2},{2,3},{4,5},{5,6},{6,7},{8,9},{9,10},{10,11},{12,13},{... | collective-permute-start | bytes 23048 | tf_op jit(solution)/shard_map/ppermute | solution.py:12
  51.4 1.9 collective-permute-start.13
  53.3 5.2 %collective-permute-start.12 = (f32[3,64,1,128]{1,3,2,0:T(8,128)S(1)}, f32[3,64,1,128]{1,3,2,0:T(8,128)S(1)}, u32[]{:S(2)}, u32[]{:S(2)}) collective-permute-start(f32[3,64,1,128]{1,3,2,0:T(8,128)S(1)} %get-tuple-element.38), channel_id=1, source_target_pairs={{0,4},{4,8},{8,12},{12,16},{16,20},{20,24},{24,28},{28,32},{32,36}... | collective-permute-start | bytes 294920 | tf_op jit(solution)/shard_map/ppermute | solution.py:12
  58.6 1.4 collective-permute-done.13
  62.5 4.5 %collective-permute-start.14 = (f32[3,64,10,1]{1,3,2,0:T(1,128)S(1)}, f32[3,64,10,1]{1,3,2,0:T(1,128)S(1)}, u32[]{:S(2)}, u32[]{:S(2)}) collective-permute-start(f32[3,64,10,1]{1,3,2,0:T(1,128)S(1)} %get-tuple-element.32), channel_id=1, source_target_pairs={{0,1},{1,2},{2,3},{4,5},{5,6},{6,7},{8,9},{9,10},{10,11},{12,13},{... | collective-permute-start | bytes 23048 | tf_op jit(solution)/shard_map/ppermute | solution.py:12
  69.5 1.7 fusion.77
  73.0 246.4 %all-reduce = (f32[64,64]{1,0:T(8,128)S(1)}, f32[64]{0:T(128)S(1)}) all-reduce(f32[64,64]{1,0:T(8,128)S(1)} %fusion.83, f32[64]{0:T(128)S(1)} %convolution_bitcast_fusion.2), channel_id=1, replica_groups=mesh['gx'=64,'gy'=4] {'gx'}, use_global_device_ids=true, to_apply=%region_2.3 | all-reduce | flops 4160 | bytes 33280 | tf_op jit(solution)/shard_map/psum | solution.py:87
  319.4 15.2 %all-reduce.1 = (f32[64,64]{1,0:T(8,128)S(1)}, f32[64]{0:T(128)S(1)}) all-reduce(f32[64,64]{1,0:T(8,128)S(1)} %get-tuple-element.5, f32[64]{0:T(128)S(1)} %get-tuple-element.6), channel_id=1, replica_groups=mesh['gx'=64,'gy'=4] {'gy'}, use_global_device_ids=true, to_apply=%region_3.4 | all-reduce | flops 4160 | bytes 33280 | tf_op jit(solution)/shard_map/psum | solution.py:87
  334.8 5.8 %cholesky.18 = f32[64,64]{1,0:T(8,128)S(1)} custom-call(f32[64,64]{1,0:T(8,128)S(1)} %fusion.74), custom_call_target="Cholesky" | custom-call | tf_op jit(solution)/shard_map/jit(cholesky)/cholesky | solution.py:88
  342.0 4.9 %custom-call.10 = f32[1,64,64]{1,2,0:T(8,128)S(1)} custom-call(f32[1,64,64]{2,1,0:T(8,128)S(1)} %fusion.70), custom_call_target="InvertDiagBlocksLowerTriangular" | custom-call | tf_op jit(solution)/shard_map/triangular_solve | solution.py:54
  347.5 2.1 fusion.15
  349.6 1.3 copy.19
  (74 shorter events, 21.6 us)
Async XLA Ops:
  1.4 8.9 %collective-permute-start.1 = (f32[2,3,128]{2,1,0:T(4,128)S(1)}, f32[2,3,128]{2,1,0:T(4,128)S(1)}, u32[]{:S(2)}, u32[]{:S(2)}) collective-permute-start(f32[2,3,128]{2,1,0:T(4,128)S(1)} %get-tuple-element.49), channel_id=1, source_target_pairs={{4,0},{8,4},{12,8},{16,12},{20,16},{24,20},{28,24},{32,28},{36,32}... | collective-permute-start | bytes 9224 | tf_op jit(solution)/shard_map/ppermute | solution.py:15
  6.5 3.8 %collective-permute-start = (f32[2,3,128]{2,1,0:T(4,128)S(1)}, f32[2,3,128]{2,1,0:T(4,128)S(1)}, u32[]{:S(2)}, u32[]{:S(2)}) collective-permute-start(f32[2,3,128]{2,1,0:T(4,128)S(1)} %get-tuple-element.48), channel_id=1, source_target_pairs={{0,4},{4,8},{8,12},{12,16},{16,20},{20,24},{24,28},{28,32},{32,36}... | collective-permute-start | bytes 9224 | tf_op jit(solution)/shard_map/ppermute | solution.py:12
  10.4 10.9 %collective-permute-start.3 = (f32[2,14,3]{2,1,0:T(8,128)S(1)}, f32[2,14,3]{2,1,0:T(8,128)S(1)}, u32[]{:S(2)}, u32[]{:S(2)}) collective-permute-start(f32[2,14,3]{2,1,0:T(8,128)S(1)} %get-tuple-element.47), channel_id=1, source_target_pairs={{1,0},{2,1},{3,2},{5,4},{6,5},{7,6},{9,8},{10,9},{11,10},{13,12},{... | collective-permute-start | bytes 1016 | tf_op jit(solution)/shard_map/ppermute | solution.py:15
  11.7 9.6 %collective-permute-start.2 = (f32[2,14,3]{2,1,0:T(8,128)S(1)}, f32[2,14,3]{2,1,0:T(8,128)S(1)}, u32[]{:S(2)}, u32[]{:S(2)}) collective-permute-start(f32[2,14,3]{2,1,0:T(8,128)S(1)} %get-tuple-element.46), channel_id=1, source_target_pairs={{0,1},{1,2},{2,3},{4,5},{5,6},{6,7},{8,9},{9,10},{10,11},{12,13},{... | collective-permute-start | bytes 1016 | tf_op jit(solution)/shard_map/ppermute | solution.py:12
  15.7 7.0 %collective-permute-start.5 = (f32[3,64,1,128]{1,3,2,0:T(8,128)S(1)}, f32[3,64,1,128]{1,3,2,0:T(8,128)S(1)}, u32[]{:S(2)}, u32[]{:S(2)}) collective-permute-start(f32[3,64,1,128]{1,3,2,0:T(8,128)S(1)} %get-tuple-element.43), channel_id=1, source_target_pairs={{4,0},{8,4},{12,8},{16,12},{20,16},{24,20},{28,24},{32,28},{36,32}... | collective-permute-start | bytes 294920 | tf_op jit(solution)/shard_map/ppermute | solution.py:15
  18.7 5.2 %collective-permute-start.4 = (f32[3,64,1,128]{1,3,2,0:T(8,128)S(1)}, f32[3,64,1,128]{1,3,2,0:T(8,128)S(1)}, u32[]{:S(2)}, u32[]{:S(2)}) collective-permute-start(f32[3,64,1,128]{1,3,2,0:T(8,128)S(1)} %get-tuple-element.42), channel_id=1, source_target_pairs={{0,4},{4,8},{8,12},{12,16},{16,20},{20,24},{24,28},{28,32},{32,36}... | collective-permute-start | bytes 294920 | tf_op jit(solution)/shard_map/ppermute | solution.py:12
  23.9 5.5 %collective-permute-start.7 = (f32[3,64,10,1]{1,3,2,0:T(1,128)S(1)}, f32[3,64,10,1]{1,3,2,0:T(1,128)S(1)}, u32[]{:S(2)}, u32[]{:S(2)}) collective-permute-start(f32[3,64,10,1]{1,3,2,0:T(1,128)S(1)} %get-tuple-element.37), channel_id=1, source_target_pairs={{1,0},{2,1},{3,2},{5,4},{6,5},{7,6},{9,8},{10,9},{11,10},{13,12},{... | collective-permute-start | bytes 23048 | tf_op jit(solution)/shard_map/ppermute | solution.py:15
  25.2 4.8 %collective-permute-start.6 = (f32[3,64,10,1]{1,3,2,0:T(1,128)S(1)}, f32[3,64,10,1]{1,3,2,0:T(1,128)S(1)}, u32[]{:S(2)}, u32[]{:S(2)}) collective-permute-start(f32[3,64,10,1]{1,3,2,0:T(1,128)S(1)} %get-tuple-element.36), channel_id=1, source_target_pairs={{0,1},{1,2},{2,3},{4,5},{5,6},{6,7},{8,9},{9,10},{10,11},{12,13},{... | collective-permute-start | bytes 23048 | tf_op jit(solution)/shard_map/ppermute | solution.py:12
  32.1 16.0 %copy-start = (s32[1,1,256]{2,1,0:T(1,128)S(1)}, s32[1,1,256]{2,1,0:T(1,128)}, u32[]{:S(2)}) copy-start(s32[1,1,256]{2,1,0:T(1,128)} %param.9) | copy-start | bytes 3076
  32.1 8.9 %collective-permute-start.9 = (f32[3,64,1,128]{1,3,2,0:T(8,128)S(1)}, f32[3,64,1,128]{1,3,2,0:T(8,128)S(1)}, u32[]{:S(2)}, u32[]{:S(2)}) collective-permute-start(f32[3,64,1,128]{1,3,2,0:T(8,128)S(1)} %get-tuple-element.41), channel_id=1, source_target_pairs={{4,0},{8,4},{12,8},{16,12},{20,16},{24,20},{28,24},{32,28},{36,32}... | collective-permute-start | bytes 294920 | tf_op jit(solution)/shard_map/ppermute | solution.py:15
  34.1 8.1 %collective-permute-start.8 = (f32[3,64,1,128]{1,3,2,0:T(8,128)S(1)}, f32[3,64,1,128]{1,3,2,0:T(8,128)S(1)}, u32[]{:S(2)}, u32[]{:S(2)}) collective-permute-start(f32[3,64,1,128]{1,3,2,0:T(8,128)S(1)} %get-tuple-element.40), channel_id=1, source_target_pairs={{0,4},{4,8},{8,12},{12,16},{16,20},{20,24},{24,28},{28,32},{32,36}... | collective-permute-start | bytes 294920 | tf_op jit(solution)/shard_map/ppermute | solution.py:12
  42.2 5.9 %collective-permute-start.11 = (f32[3,64,10,1]{1,3,2,0:T(1,128)S(1)}, f32[3,64,10,1]{1,3,2,0:T(1,128)S(1)}, u32[]{:S(2)}, u32[]{:S(2)}) collective-permute-start(f32[3,64,10,1]{1,3,2,0:T(1,128)S(1)} %get-tuple-element.35), channel_id=1, source_target_pairs={{1,0},{2,1},{3,2},{5,4},{6,5},{7,6},{9,8},{10,9},{11,10},{13,12},{... | collective-permute-start | bytes 23048 | tf_op jit(solution)/shard_map/ppermute | solution.py:15
  43.5 5.4 %collective-permute-start.10 = (f32[3,64,10,1]{1,3,2,0:T(1,128)S(1)}, f32[3,64,10,1]{1,3,2,0:T(1,128)S(1)}, u32[]{:S(2)}, u32[]{:S(2)}) collective-permute-start(f32[3,64,10,1]{1,3,2,0:T(1,128)S(1)} %get-tuple-element.34), channel_id=1, source_target_pairs={{0,1},{1,2},{2,3},{4,5},{5,6},{6,7},{8,9},{9,10},{10,11},{12,13},{... | collective-permute-start | bytes 23048 | tf_op jit(solution)/shard_map/ppermute | solution.py:12
  51.4 8.6 %collective-permute-start.13 = (f32[3,64,1,128]{1,3,2,0:T(8,128)S(1)}, f32[3,64,1,128]{1,3,2,0:T(8,128)S(1)}, u32[]{:S(2)}, u32[]{:S(2)}) collective-permute-start(f32[3,64,1,128]{1,3,2,0:T(8,128)S(1)} %get-tuple-element.39), channel_id=1, source_target_pairs={{4,0},{8,4},{12,8},{16,12},{20,16},{24,20},{28,24},{32,28},{36,32}... | collective-permute-start | bytes 294920 | tf_op jit(solution)/shard_map/ppermute | solution.py:15
  53.3 7.8 %collective-permute-start.12 = (f32[3,64,1,128]{1,3,2,0:T(8,128)S(1)}, f32[3,64,1,128]{1,3,2,0:T(8,128)S(1)}, u32[]{:S(2)}, u32[]{:S(2)}) collective-permute-start(f32[3,64,1,128]{1,3,2,0:T(8,128)S(1)} %get-tuple-element.38), channel_id=1, source_target_pairs={{0,4},{4,8},{8,12},{12,16},{16,20},{20,24},{24,28},{28,32},{32,36}... | collective-permute-start | bytes 294920 | tf_op jit(solution)/shard_map/ppermute | solution.py:12
  61.2 5.9 %collective-permute-start.15 = (f32[3,64,10,1]{1,3,2,0:T(1,128)S(1)}, f32[3,64,10,1]{1,3,2,0:T(1,128)S(1)}, u32[]{:S(2)}, u32[]{:S(2)}) collective-permute-start(f32[3,64,10,1]{1,3,2,0:T(1,128)S(1)} %get-tuple-element.33), channel_id=1, source_target_pairs={{1,0},{2,1},{3,2},{5,4},{6,5},{7,6},{9,8},{10,9},{11,10},{13,12},{... | collective-permute-start | bytes 23048 | tf_op jit(solution)/shard_map/ppermute | solution.py:15
  62.5 5.4 %collective-permute-start.14 = (f32[3,64,10,1]{1,3,2,0:T(1,128)S(1)}, f32[3,64,10,1]{1,3,2,0:T(1,128)S(1)}, u32[]{:S(2)}, u32[]{:S(2)}) collective-permute-start(f32[3,64,10,1]{1,3,2,0:T(1,128)S(1)} %get-tuple-element.32), channel_id=1, source_target_pairs={{0,1},{1,2},{2,3},{4,5},{5,6},{6,7},{8,9},{9,10},{10,11},{12,13},{... | collective-permute-start | bytes 23048 | tf_op jit(solution)/shard_map/ppermute | solution.py:12
  71.3 1.0 copy-start.1
  71.3 1.0 copy-start.2
